TPU v7x, 32 devices: a whole 2x2x4 slice. The times are simulated.
32 devices in a mesh: wide: 8 (over y, x, core), by: 4 (over z).
Axes of the slice: x: 2, y: 2, z: 4, core: 2. Of those that a mesh axis runs over, the one named last changes fastest.
Arguments:
- tiles: float32 [704, 512, 512], P(('wide', 'by')), may hold values from -6 to 6
- tile_rows: int32 [704], P(('wide', 'by')), may hold values from 0 to 7
- tile_cols: int32 [704], P(('wide', 'by')), may hold values from 0 to 63, as said below
- start_panel: float32 [32768, 64], P('wide'), may hold values from -6 to 6
Outputs:
- panel: float32 [32768, 64], P('wide')
- factor: float32 [64, 64], replicated
Inputs may be any that keep to these rules, and one draw needn't show every extreme that they name: `tile_cols`: within one device's 22 tiles, at most 3 have block columns in the block rows of one index of wide, and one index of wide takes exactly 3 of them.
All inputs are finite; a program needn't handle non-finite values.
Results may differ from a plain program's by a relative error of at most 0.0001.
Values sent between devices are 32-bit elements; how exact they have to be, the bound alone decides.
No kernel may reach another device: no remote copies, remote signals or barrier semaphores. Data moves between devices by JAX's collectives and lax.ppermute only.
A program may use at most 192 MiB of HBM per device.

v0:
```python
import jax
import jax.numpy as jnp
from jax import lax
from jax.sharding import PartitionSpec as P

ITERS = 2


def local(tiles, tile_rows, tile_cols, start_panel):
    wide_count = lax.axis_size("wide")
    my_wide = lax.axis_index("wide")
    tile_count = tiles.shape[0]
    block_size = tiles.shape[1]
    width = start_panel.shape[1]
    block_rows = start_panel.shape[0] // block_size
    capacity = max(2, tile_count // wide_count + 1)
    slot_count = wide_count * capacity
    highest = lax.Precision.HIGHEST
    peer_index = tile_cols // block_rows
    positions = jnp.arange(tile_count, dtype=jnp.int32)
    earlier = positions[:, None] > positions[None, :]
    same_peer = peer_index[:, None] == peer_index[None, :]
    rank_within = jnp.sum((earlier & same_peer).astype(jnp.int32), axis=1)
    slot_of = peer_index * capacity + rank_within
    slot_match = slot_of[:, None] == jnp.arange(slot_count, dtype=jnp.int32)[None, :]
    slot_table = slot_match.astype(jnp.float32)
    request = jnp.sum(jnp.where(slot_match, tile_cols[:, None] + 1, 0), axis=0) - 1
    incoming = lax.all_to_all(
        request.reshape(wide_count, capacity), "wide", split_axis=0, concat_axis=0, tiled=True
    ).reshape(slot_count)
    local_in = incoming - my_wide * block_rows
    block_iota = jnp.arange(block_rows, dtype=jnp.int32)
    serve_table = (local_in[:, None] == block_iota[None, :]).astype(jnp.float32)
    row_table = (tile_rows[:, None] == block_iota[None, :]).astype(jnp.float32)
    panel = start_panel
    factor = jnp.zeros((width, width), jnp.float32)
    for step in range(ITERS):
        flat_panel = panel.reshape(block_rows, block_size * width)
        outgoing = jnp.dot(serve_table, flat_panel, precision=highest)
        received = lax.all_to_all(outgoing, "wide", split_axis=0, concat_axis=0, tiled=True)
        col_panels = jnp.dot(slot_table, received, precision=highest).reshape(
            tile_count, block_size, width
        )
        row_panels = jnp.dot(row_table, flat_panel, precision=highest).reshape(
            tile_count, block_size, width
        )
        direct = jnp.einsum("tab,tbk->tak", tiles, col_panels, precision=highest)
        mirror = jnp.einsum("tba,tbk->tak", tiles, row_panels, precision=highest)
        partial_rows = jnp.dot(
            row_table.T, direct.reshape(tile_count, block_size * width), precision=highest
        )
        mirror_flat = mirror.reshape(tile_count, block_size * width)
        placed = jnp.dot(slot_table.T, mirror_flat, precision=highest)
        returned = lax.all_to_all(placed, "wide", split_axis=0, concat_axis=0, tiled=True)
        partial_rows = partial_rows + jnp.dot(serve_table.T, returned, precision=highest)
        partial_rows = partial_rows.reshape(block_rows * block_size, width)
        image = lax.psum(partial_rows, "by")
        gram = lax.psum(jnp.dot(image.T, image, precision=highest), "wide")
        factor = jnp.linalg.cholesky(gram)
        panel = jax.scipy.linalg.solve_triangular(factor, image.T, lower=True).T
    return (panel, factor)


def solution(mesh):
    placed = (P(("wide", "by"), None, None), P(("wide", "by")), P(("wide", "by")), P("wide", None))
    return jax.shard_map(
        local, mesh=mesh, in_specs=placed, out_specs=(P("wide", None), P()), check_vma=False
    )
```

profile of v0, /device:TPU:0, one launch (start us, length us, event | category | flops | bytes accessed | tf_op | source)
XLA Modules:
  0.0 638.6 jit_solution(3037137050593948503)
XLA Ops:
  8.8 5.2 all-to-all-start
  22.6 21.3 %fusion.13 = f32[22,512,64]{1,2,0:T(8,128)} fusion(f32[22,512,512]{2,1,0:T(8,128)} %param.7, f32[22,512,64]{1,0,2:T(8,128)S(1)} %fusion.60), kind=kOutput, calls=%fused_computation.15 | convolution fusion | flops 4429185024 | bytes 28835840 | tf_op jit(solution)/shard_map/tba,tbk->tak/dot_general | solution.py:48
  43.9 5.3 copy.59
  49.2 6.3 reshape.153
  63.2 4.5 all-to-all-start.2
  75.3 41.6 %all-to-all-done.2 = f32[8,3,32768]{2,1,0:T(4,128)} async-done(((f32[8,3,32768]{2,1,0:T(4,128)}), f32[8,3,32768]{2,1,0:T(4,128)}, u32[]{:S(2)}, u32[]{:S(2)}) %all-to-all-start.2) | async-done | bytes 3145760 | tf_op jit(solution)/shard_map/all_to_all | solution.py:54
  116.9 4.5 all-to-all-start.1
  125.3 45.2 %all-to-all-done.1 = f32[8,3,32768]{2,1,0:T(4,128)} async-done(((f32[8,3,32768]{2,1,0:T(4,128)}), f32[8,3,32768]{2,1,0:T(4,128)}, u32[]{:S(2)}, u32[]{:S(2)}) %all-to-all-start.1) | async-done | bytes 3145760 | tf_op jit(solution)/shard_map/all_to_all | solution.py:40
  170.5 5.5 all_to_all.30
  176.0 6.4 %dot_general.80 = f32[512,64,24]{1,0,2:T(8,128)} reshape(f32[32768,24]{0,1:T(8,128)} %bitcast.82) | data formatting | bytes 6291456 | tf_op jit(solution)/shard_map/dot_general | solution.py:41
  182.4 6.6 %copy.54 = f32[512,64,24]{0,2,1:T(8,128)} copy(f32[512,64,24]{1,0,2:T(8,128)} %dot_general.80) | data formatting | bytes 6291456 | tf_op jit(solution)/shard_map/dot_general | solution.py:41
  192.6 27.3 %fusion.10 = f32[22,512,64]{1,2,0:T(8,128)} fusion(f32[22,512,512]{2,1,0:T(8,128)} %param.7, f32[22,512,64]{1,0,2:T(8,128)S(1)} %fusion.37), kind=kOutput, calls=%fused_computation.14 | convolution fusion | flops 4429185024 | bytes 28835840 | tf_op jit(solution)/shard_map/tab,tbk->tak/dot_general | solution.py:47
  219.9 5.3 copy.56
  225.3 6.5 %reshape.143 = f32[22,32768]{1,0:T(8,128)} reshape(f32[22,512,64]{2,1,0:T(8,128)} %copy.56) | data formatting | bytes 5767168 | tf_op jit(solution)/shard_map/reshape | solution.py:50
  240.5 86.1 %all-reduce.3.cloned.1.call-done = f32[4096,64]{1,0:T(8,128)} async-done(((f32[4096,64]{1,0:T(8,128)}), f32[4096,64]{1,0:T(8,128)}) %all-reduce.3.cloned.1.call-update) | async-done | bytes 1048592 | tf_op jit(solution)/shard_map/psum | solution.py:57
  326.6 5.9 fusion.68
  332.5 24.3 %psum.29 = f32[64,64]{0,1:T(8,128)S(1)} all-reduce(f32[64,64]{0,1:T(8,128)S(1)} %fusion.68), channel_id=1, replica_groups=mesh['wide'=8,'by'=4] {'wide'}, use_global_device_ids=true, to_apply=%region_3.4 | all-reduce | flops 4096 | bytes 32768 | tf_op jit(solution)/shard_map/psum | solution.py:58
  356.9 5.8 cholesky.44
  364.1 4.9 custom-call.6
  378.2 4.8 all-to-all-start.3
  386.9 19.4 %fusion.19 = f32[22,512,64]{1,2,0:T(8,128)S(1)} fusion(f32[22,512,512]{2,1,0:T(8,128)} %param.7, f32[22,512,64]{1,0,2:T(8,128)S(1)} %fusion.58), kind=kOutput, calls=%fused_computation.17 | convolution fusion | flops 4429185024 | bytes 28835840 | tf_op jit(solution)/shard_map/tba,tbk->tak/dot_general | solution.py:48
  410.2 4.6 reshape.155
  420.5 11.6 %all-to-all-done.3 = f32[8,3,32768]{2,1,0:T(4,128)} async-done(((f32[8,3,32768]{2,1,0:T(4,128)}), f32[8,3,32768]{2,1,0:T(4,128)}, u32[]{:S(2)}, u32[]{:S(2)}) %all-to-all-start.3) | async-done | bytes 3145760 | tf_op jit(solution)/shard_map/all_to_all | solution.py:40
  432.2 4.5 all-to-all-start.4
  440.5 4.9 dot_general.95
  445.4 5.0 copy.65
  452.1 25.6 %fusion.16 = f32[22,512,64]{1,2,0:T(8,128)S(1)} fusion(f32[22,512,512]{2,1,0:T(8,128)} %param.7, f32[22,512,64]{1,0,2:T(8,128)S(1)} %fusion.35), kind=kOutput, calls=%fused_computation.16 | convolution fusion | flops 4429185024 | bytes 28835840 | tf_op jit(solution)/shard_map/tab,tbk->tak/dot_general | solution.py:47
  498.9 86.2 %all-reduce.5.cloned.1.call-done = f32[4096,64]{1,0:T(8,128)} async-done(((f32[4096,64]{1,0:T(8,128)}), f32[4096,64]{1,0:T(8,128)}) %all-reduce.5.cloned.1.call-update) | async-done | bytes 1048592 | tf_op jit(solution)/shard_map/psum | solution.py:57
  585.1 5.9 fusion.69
  591.0 24.4 %psum.31 = f32[64,64]{0,1:T(8,128)S(1)} all-reduce(f32[64,64]{0,1:T(8,128)S(1)} %fusion.69), channel_id=1, replica_groups=mesh['wide'=8,'by'=4] {'wide'}, use_global_device_ids=true, to_apply=%region_7.10 | all-reduce | flops 4096 | bytes 32768 | tf_op jit(solution)/shard_map/psum | solution.py:58
  615.5 5.8 cholesky.55
  623.3 4.9 custom-call.7
  (69 shorter events, 97.6 us)
Async XLA Ops:
  8.8 54.4 %all-to-all-start = ((s32[8,1,3]{2,1,0:T(1,128)}), s32[8,1,3]{2,1,0:T(1,128)S(1)}, u32[]{:S(2)}, u32[]{:S(2)}) async-start(s32[8,1,3]{2,1,0:T(1,128)} %bitcast.1), calls=%async_computation | async-start | bytes 8192 | tf_op jit(solution)/shard_map/all_to_all | solution.py:28
  16.5 4.7 copy-start.2
  63.2 53.7 %all-to-all-start.2 = ((f32[8,3,32768]{2,1,0:T(4,128)}), f32[8,3,32768]{2,1,0:T(4,128)}, u32[]{:S(2)}, u32[]{:S(2)}) async-start(f32[8,3,32768]{2,1,0:T(4,128)} %copy.60), calls=%async_computation.2 | async-start | bytes 8388608 | tf_op jit(solution)/shard_map/all_to_all | solution.py:54
  116.9 53.7 %all-to-all-start.1 = ((f32[8,3,32768]{2,1,0:T(4,128)}), f32[8,3,32768]{2,1,0:T(4,128)}, u32[]{:S(2)}, u32[]{:S(2)}) async-start(f32[8,3,32768]{2,1,0:T(4,128)} %copy.53), calls=%async_computation.1 | async-start | bytes 8388608 | tf_op jit(solution)/shard_map/all_to_all | solution.py:40
  121.4 205.1 %all-reduce.3.cloned.1.call-start = ((), (), s32[]{:S(2)}) async-start(), calls=%async_computation.5 | async-start | bytes 4194304 | tf_op jit(solution)/shard_map/psum | solution.py:57
  326.6 42.5 %copy-start.1 = (f32[4096,64]{1,0:T(8,128)S(1)}, f32[4096,64]{1,0:T(8,128)}, u32[]{:S(2)}) copy-start(f32[4096,64]{1,0:T(8,128)} %all-reduce.3.cloned.1.call-done) | copy-start | bytes 3145732
  378.2 54.0 %all-to-all-start.3 = ((f32[8,3,32768]{2,1,0:T(4,128)}), f32[8,3,32768]{2,1,0:T(4,128)}, u32[]{:S(2)}, u32[]{:S(2)}) async-start(f32[8,3,32768]{2,1,0:T(4,128)} %copy.64), calls=%async_computation.3 | async-start | bytes 8388608 | tf_op jit(solution)/shard_map/all_to_all | solution.py:40
  432.2 56.1 %all-to-all-start.4 = ((f32[8,3,32768]{2,1,0:T(4,128)}), f32[8,3,32768]{2,1,0:T(4,128)}, u32[]{:S(2)}, u32[]{:S(2)}) async-start(f32[8,3,32768]{2,1,0:T(4,128)} %copy.71), calls=%async_computation.4 | async-start | bytes 8388608 | tf_op jit(solution)/shard_map/all_to_all | solution.py:54
  436.7 148.4 %all-reduce.5.cloned.1.call-start = ((), (), s32[]{:S(2)}) async-start(), calls=%async_computation.6 | async-start | bytes 4194304 | tf_op jit(solution)/shard_map/psum | solution.py:57
  585.1 43.1 %copy-start = (f32[4096,64]{1,0:T(8,128)S(1)}, f32[4096,64]{1,0:T(8,128)}, u32[]{:S(2)}) copy-start(f32[4096,64]{1,0:T(8,128)} %all-reduce.5.cloned.1.call-done) | copy-start | bytes 3145732
Sparse Core Ops, SparseCore 0:
  240.6 85.9 all-reduce.2
  499.0 86.0 all-reduce.4
where the time goes:
time: 648 us; the launch traced here: 639 us
  waiting for transfers between devices  271 us (42%)
  matrix products  138 us (21%)
  local copies, waits for them, and re-layouts  116 us (18%)
  blocking collectives  48.7 us (8%)
  other arithmetic  26.4 us (4%)
  starting transfers between devices  23.7 us (4%)
  between operations  14.6 us (2%)
    psum x2, waiting for transfers between devices, local(): image = lax.psum(partial_rows, 'by')  172 us
    all_to_all x2, waiting for transfers between devices, local(): lax.all_to_all(outgoing, 'wide', split_axis=0, concat_axis=0, tiled=True)  56.9 us
    dot_general x2, matrix products, local(): direct = jnp.einsum('tab,tbk->tak', tiles, col_panels, precision=highest)  52.9 us
    psum x2, blocking collectives, local(): gram = lax.psum(jnp.dot(image.T, image, precision=highest), 'wide')  48.7 us
    all_to_all x2, waiting for transfers between devices, local(): lax.all_to_all(placed, 'wide', split_axis=0, concat_axis=0, tiled=True)  41.6 us
    dot_general x2, matrix products, local(): mirror = jnp.einsum('tba,tbk->tak', tiles, row_panels, precision=highest)  40.7 us
    dot_general x4, local copies, waits for them, and re-layouts, local(): jnp.dot(slot_table, received, precision=highest)  22.9 us
    another operation x6, other arithmetic, local(): factor = jnp.linalg.cholesky(gram)  13 us
  transfers between devices with their start and end apart: 7, of which 5 were waited for; matrix products, arithmetic and copies ran while one was open for 22% of the time, Pallas kernels for 0%

commit v1 on v0

--- a/solution.py
+++ b/solution.py
@@ -54,7 +54,10 @@
         returned = lax.all_to_all(placed, "wide", split_axis=0, concat_axis=0, tiled=True)
         partial_rows = partial_rows + jnp.dot(serve_table.T, returned, precision=highest)
         partial_rows = partial_rows.reshape(block_rows * block_size, width)
-        image = lax.psum(partial_rows, "by")
+        ndev = jax.lax.psum(1, axis_name="by")
+        image = partial_rows
+        for i in [[(it, it ^ kk) for it in range(ndev)] for kk in (1, 2, 4, 8, 16) if kk < ndev]:
+            image = image + jax.lax.ppermute(image, perm=i, axis_name="by")
         gram = lax.psum(jnp.dot(image.T, image, precision=highest), "wide")
         factor = jnp.linalg.cholesky(gram)
         panel = jax.scipy.linalg.solve_triangular(factor, image.T, lower=True).T

time: 648 us -> 627 us (0.968)
  waiting for transfers between devices: 271 us -> 231 us
  between operations: 14.6 us -> 1.18 us
  local copies, waits for them, and re-layouts: 116 us -> 127 us
  starting transfers between devices: 23.7 us -> 33.6 us
    psum x2 -> x0, waiting for transfers between devices: 172 us -> none  [local(): image = lax.psum(partial_rows, 'by')]
    ppermute x0 -> x4, waiting for transfers between devices: none -> 132 us  [local(): image = image + jax.lax.ppermute(image, perm=i, axis_name='by')]
    ppermute x0 -> x4, starting transfers between devices: none -> 9.31 us  [local(): image = image + jax.lax.ppermute(image, perm=i, axis_name='by')]
    ppermute x0 -> x4, local copies, waits for them, and re-layouts: none -> 7.73 us  [local(): image = image + jax.lax.ppermute(image, perm=i, axis_name='by')]
  transfers between devices with their start and end apart: 7 -> 9, of which waited for: 5 -> 7; matrix products, arithmetic and copies ran while one was open for 22% -> 23% of each run, Pallas kernels for 0% -> 0%
where the time goes in v1:
time: 627 us; the launch traced here: 617 us
  waiting for transfers between devices  231 us (37%)
  matrix products  142 us (23%)
  local copies, waits for them, and re-layouts  127 us (20%)
  blocking collectives  51.3 us (8%)
  starting transfers between devices  33.6 us (5%)
  other arithmetic  31.3 us (5%)
    ppermute x4, waiting for transfers between devices, local(): image = image + jax.lax.ppermute(image, perm=i, axis_name='by')  132 us
    all_to_all x2, waiting for transfers between devices, local(): lax.all_to_all(outgoing, 'wide', split_axis=0, concat_axis=0, tiled=True)  57.2 us
    dot_general x2, matrix products, local(): direct = jnp.einsum('tab,tbk->tak', tiles, col_panels, precision=highest)  53 us
    psum x2, blocking collectives, local(): gram = lax.psum(jnp.dot(image.T, image, precision=highest), 'wide')  51.3 us
    all_to_all x2, waiting for transfers between devices, local(): lax.all_to_all(placed, 'wide', split_axis=0, concat_axis=0, tiled=True)  41.6 us
    dot_general x2, matrix products, local(): mirror = jnp.einsum('tba,tbk->tak', tiles, row_panels, precision=highest)  40.7 us
    dot_general x4, local copies, waits for them, and re-layouts, local(): jnp.dot(slot_table, received, precision=highest)  22.3 us
    another operation x6, other arithmetic, local(): factor = jnp.linalg.cholesky(gram)  13 us
  transfers between devices with their start and end apart: 9, of which 7 were waited for; matrix products, arithmetic and copies ran while one was open for 23% of the time, Pallas kernels for 0%

profile of v1, /device:TPU:0, one launch (start us, length us, event | category | flops | bytes accessed | tf_op | source)
XLA Modules:
  0.0 617.1 jit_solution(1070326861681144036)
XLA Ops:
  2.3 5.2 all-to-all-start
  16.1 21.3 %fusion.13 = f32[22,512,64]{1,2,0:T(8,128)} fusion(f32[22,512,512]{2,1,0:T(8,128)} %param.7, f32[22,512,64]{1,0,2:T(8,128)S(1)} %fusion.66), kind=kOutput, calls=%fused_computation.15 | convolution fusion | flops 4429185024 | bytes 28835840 | tf_op jit(solution)/shard_map/tba,tbk->tak/dot_general | solution.py:48
  37.4 5.3 copy.67
  42.7 6.4 %reshape.153 = f32[22,32768,1]{1,0,2:T(8,128)} reshape(f32[22,512,64]{2,1,0:T(8,128)} %copy.67) | data formatting | bytes 5767168 | tf_op jit(solution)/shard_map/reshape | solution.py:52
  68.8 41.6 %all-to-all-done.2 = f32[8,3,32768]{2,1,0:T(4,128)} async-done(((f32[8,3,32768]{2,1,0:T(4,128)}), f32[8,3,32768]{2,1,0:T(4,128)}, u32[]{:S(2)}, u32[]{:S(2)}) %all-to-all-start.2) | async-done | bytes 3145760 | tf_op jit(solution)/shard_map/all_to_all | solution.py:54
  110.5 5.1 all-to-all-start.1
  119.4 45.3 %all-to-all-done.1 = f32[8,3,32768]{2,1,0:T(4,128)} async-done(((f32[8,3,32768]{2,1,0:T(4,128)}), f32[8,3,32768]{2,1,0:T(4,128)}, u32[]{:S(2)}, u32[]{:S(2)}) %all-to-all-start.1) | async-done | bytes 3145760 | tf_op jit(solution)/shard_map/all_to_all | solution.py:40
  164.7 5.5 all_to_all.30
  170.1 6.2 %dot_general.80 = f32[512,64,24]{1,0,2:T(8,128)} reshape(f32[32768,24]{0,1:T(8,128)} %bitcast.78) | data formatting | bytes 6291456 | tf_op jit(solution)/shard_map/dot_general | solution.py:41
  176.3 6.6 %copy.62 = f32[512,64,24]{0,2,1:T(8,128)} copy(f32[512,64,24]{1,0,2:T(8,128)} %dot_general.80) | data formatting | bytes 6291456 | tf_op jit(solution)/shard_map/dot_general | solution.py:41
  186.5 27.5 %fusion.10 = f32[22,512,64]{1,2,0:T(8,128)} fusion(f32[22,512,512]{2,1,0:T(8,128)} %param.7, f32[22,512,64]{1,0,2:T(8,128)S(1)} %fusion.43), kind=kOutput, calls=%fused_computation.14 | convolution fusion | flops 4429185024 | bytes 28835840 | tf_op jit(solution)/shard_map/tab,tbk->tak/dot_general | solution.py:47
  214.0 5.3 copy.64
  219.4 6.3 %reshape.143 = f32[22,32768]{1,0:T(8,128)} reshape(f32[22,512,64]{2,1,0:T(8,128)} %copy.64) | data formatting | bytes 5767168 | tf_op jit(solution)/shard_map/reshape | solution.py:50
  236.3 20.6 %collective-permute-done = f32[4096,64]{0,1:T(8,128)S(1)} collective-permute-done((f32[4096,64]{0,1:T(8,128)}, f32[4096,64]{0,1:T(8,128)S(1)}, u32[]{:S(2)}, u32[]{:S(2)}) %collective-permute-start) | collective-permute-done | bytes 1048608 | tf_op jit(solution)/shard_map/ppermute | solution.py:60
  265.4 42.0 %collective-permute-done.1 = f32[4096,64]{0,1:T(8,128)S(1)} collective-permute-done((f32[4096,64]{0,1:T(8,128)}, f32[4096,64]{0,1:T(8,128)S(1)}, u32[]{:S(2)}, u32[]{:S(2)}) %collective-permute-start.1) | collective-permute-done | bytes 1048608 | tf_op jit(solution)/shard_map/ppermute | solution.py:60
  309.4 5.9 fusion.26
  315.2 27.6 %psum.14 = f32[64,64]{0,1:T(8,128)S(1)} all-reduce(f32[64,64]{0,1:T(8,128)S(1)} %fusion.26), channel_id=1, replica_groups=mesh['wide'=8,'by'=4] {'wide'}, use_global_device_ids=true, to_apply=%region_2.3 | all-reduce | flops 4096 | bytes 32768 | tf_op jit(solution)/shard_map/psum | solution.py:61
  343.0 5.8 cholesky.44
  350.2 4.9 custom-call.6
  365.9 4.8 all-to-all-start.3
  374.5 19.4 %fusion.19 = f32[22,512,64]{1,2,0:T(8,128)S(1)} fusion(f32[22,512,512]{2,1,0:T(8,128)} %param.7, f32[22,512,64]{1,0,2:T(8,128)S(1)} %fusion.64), kind=kOutput, calls=%fused_computation.17 | convolution fusion | flops 4429185024 | bytes 28835840 | tf_op jit(solution)/shard_map/tba,tbk->tak/dot_general | solution.py:48
  407.9 11.9 %all-to-all-done.3 = f32[8,3,32768]{2,1,0:T(4,128)} async-done(((f32[8,3,32768]{2,1,0:T(4,128)}), f32[8,3,32768]{2,1,0:T(4,128)}, u32[]{:S(2)}, u32[]{:S(2)}) %all-to-all-start.3) | async-done | bytes 3145760 | tf_op jit(solution)/shard_map/all_to_all | solution.py:40
  419.8 4.8 all-to-all-start.4
  432.8 5.0 copy.77
  439.5 25.6 %fusion.16 = f32[22,512,64]{1,2,0:T(8,128)S(1)} fusion(f32[22,512,512]{2,1,0:T(8,128)} %param.7, f32[22,512,64]{1,0,2:T(8,128)S(1)} %fusion.41), kind=kOutput, calls=%fused_computation.16 | convolution fusion | flops 4429185024 | bytes 28835840 | tf_op jit(solution)/shard_map/tab,tbk->tak/dot_general | solution.py:47
  488.7 24.0 %collective-permute-done.2 = f32[4096,64]{0,1:T(8,128)S(1)} collective-permute-done((f32[4096,64]{0,1:T(8,128)}, f32[4096,64]{0,1:T(8,128)S(1)}, u32[]{:S(2)}, u32[]{:S(2)}) %collective-permute-start.2) | collective-permute-done | bytes 1048608 | tf_op jit(solution)/shard_map/ppermute | solution.py:60
  521.8 45.9 %collective-permute-done.3 = f32[4096,64]{0,1:T(8,128)S(1)} collective-permute-done((f32[4096,64]{0,1:T(8,128)}, f32[4096,64]{0,1:T(8,128)S(1)}, u32[]{:S(2)}, u32[]{:S(2)}) %collective-permute-start.3) | collective-permute-done | bytes 1048608 | tf_op jit(solution)/shard_map/ppermute | solution.py:60
  569.6 5.9 fusion.23
  575.5 23.6 %psum.15 = f32[64,64]{0,1:T(8,128)S(1)} all-reduce(f32[64,64]{0,1:T(8,128)S(1)} %fusion.23), channel_id=1, replica_groups=mesh['wide'=8,'by'=4] {'wide'}, use_global_device_ids=true, to_apply=%region_5.8 | all-reduce | flops 4096 | bytes 32768 | tf_op jit(solution)/shard_map/psum | solution.py:61
  599.2 5.8 cholesky.55
  607.0 4.9 custom-call.7
  611.9 4.9 convolution_bitcast_fusion
  (81 shorter events, 135.2 us)
Async XLA Ops:
  2.3 54.5 %all-to-all-start = ((s32[8,1,3]{2,1,0:T(1,128)}), s32[8,1,3]{2,1,0:T(1,128)S(1)}, u32[]{:S(2)}, u32[]{:S(2)}) async-start(s32[8,1,3]{2,1,0:T(1,128)} %bitcast.1), calls=%async_computation | async-start | bytes 8192 | tf_op jit(solution)/shard_map/all_to_all | solution.py:28
  9.9 4.7 copy-start.2
  56.8 53.7 %all-to-all-start.2 = ((f32[8,3,32768]{2,1,0:T(4,128)}), f32[8,3,32768]{2,1,0:T(4,128)}, u32[]{:S(2)}, u32[]{:S(2)}) async-start(f32[8,3,32768]{2,1,0:T(4,128)} %copy.68), calls=%async_computation.2 | async-start | bytes 8388608 | tf_op jit(solution)/shard_map/all_to_all | solution.py:54
  110.5 54.2 %all-to-all-start.1 = ((f32[8,3,32768]{2,1,0:T(4,128)}), f32[8,3,32768]{2,1,0:T(4,128)}, u32[]{:S(2)}, u32[]{:S(2)}) async-start(f32[8,3,32768]{2,1,0:T(4,128)} %copy.61), calls=%async_computation.1 | async-start | bytes 8388608 | tf_op jit(solution)/shard_map/all_to_all | solution.py:40
  233.1 23.8 %copy-start = (f32[4096,64]{1,0:T(8,128)}, f32[4096,64]{1,0:T(8,128)S(1)}, u32[]{:S(2)}) copy-start(f32[4096,64]{1,0:T(8,128)S(1)} %reshape.145) | copy-start | bytes 3145732
  234.8 22.1 %collective-permute-start = (f32[4096,64]{0,1:T(8,128)}, f32[4096,64]{0,1:T(8,128)S(1)}, u32[]{:S(2)}, u32[]{:S(2)}) collective-permute-start(f32[4096,64]{0,1:T(8,128)} %copy.69), channel_id=1, source_target_pairs={{0,1},{1,0},{2,3},{3,2},{4,5},{5,4},{6,7},{7,6},{8,9},{9,8},{10,11... | collective-permute-start | bytes 3145736 | tf_op jit(solution)/shard_map/ppermute | solution.py:60
  262.8 44.6 %collective-permute-start.1 = (f32[4096,64]{0,1:T(8,128)}, f32[4096,64]{0,1:T(8,128)S(1)}, u32[]{:S(2)}, u32[]{:S(2)}) collective-permute-start(f32[4096,64]{0,1:T(8,128)} %copy.71), channel_id=1, source_target_pairs={{0,2},{1,3},{2,0},{3,1},{4,6},{5,7},{6,4},{7,5},{8,10},{9,11},{10,... | collective-permute-start | bytes 3145736 | tf_op jit(solution)/shard_map/ppermute | solution.py:60
  365.9 53.9 %all-to-all-start.3 = ((f32[8,3,32768]{2,1,0:T(4,128)}), f32[8,3,32768]{2,1,0:T(4,128)}, u32[]{:S(2)}, u32[]{:S(2)}) async-start(f32[8,3,32768]{2,1,0:T(4,128)} %copy.76), calls=%async_computation.3 | async-start | bytes 8388608 | tf_op jit(solution)/shard_map/all_to_all | solution.py:40
  419.8 56.1 %all-to-all-start.4 = ((f32[8,3,32768]{2,1,0:T(4,128)}), f32[8,3,32768]{2,1,0:T(4,128)}, u32[]{:S(2)}, u32[]{:S(2)}) async-start(f32[8,3,32768]{2,1,0:T(4,128)} %copy.83), calls=%async_computation.4 | async-start | bytes 8388608 | tf_op jit(solution)/shard_map/all_to_all | solution.py:54
  485.1 27.5 %copy-start.1 = (f32[4096,64]{1,0:T(8,128)}, f32[4096,64]{1,0:T(8,128)S(1)}, u32[]{:S(2)}) copy-start(f32[4096,64]{1,0:T(8,128)S(1)} %reshape.149) | copy-start | bytes 3145732
  486.8 25.8 %collective-permute-start.2 = (f32[4096,64]{0,1:T(8,128)}, f32[4096,64]{0,1:T(8,128)S(1)}, u32[]{:S(2)}, u32[]{:S(2)}) collective-permute-start(f32[4096,64]{0,1:T(8,128)} %copy.84), channel_id=1, source_target_pairs={{0,1},{1,0},{2,3},{3,2},{4,5},{5,4},{6,7},{7,6},{8,9},{9,8},{10,11... | collective-permute-start | bytes 3145736 | tf_op jit(solution)/shard_map/ppermute | solution.py:60
  518.5 49.1 %collective-permute-start.3 = (f32[4096,64]{0,1:T(8,128)}, f32[4096,64]{0,1:T(8,128)S(1)}, u32[]{:S(2)}, u32[]{:S(2)}) collective-permute-start(f32[4096,64]{0,1:T(8,128)} %copy.86), channel_id=1, source_target_pairs={{0,2},{1,3},{2,0},{3,1},{4,6},{5,7},{6,4},{7,5},{8,10},{9,11},{10,... | collective-permute-start | bytes 3145736 | tf_op jit(solution)/shard_map/ppermute | solution.py:60
